TPU v7x, 32 devices: a whole 2x2x4 slice. The times are simulated.
32 devices in a mesh: lat: 8 (over z, y), lon: 4 (over x, core).
Axes of the slice: x: 2, y: 2, z: 4, core: 2. Of those that a mesh axis runs over, the one named last changes fastest.
Arguments:
- grid_field: float32 [384, 64, 512], P(None, 'lat', 'lon'), may hold values from -6 to 6
- disco_dlat: int32 [64, 16], P('lat'), may hold values from -2 to 2
- disco_dlon: int32 [64, 16], P('lat'), may hold values from -2 to 2
- disco_basis: int32 [64, 16], P('lat'), may hold values from 0 to 3
- disco_quad: float32 [64, 16], P('lat'), may hold values from 0.05 to 0.5
- disco_weight: bfloat16 [4, 384, 384], replicated, may hold values from -0.3125 to 0.3125
- norm_gain: float32 [384], replicated, may hold values from 0.1 to 1.9
- spectral_filter: float32 [384, 64], replicated, may hold values from -6 to 6
- mix_weight: bfloat16 [384, 384], replicated, may hold values from -0.3125 to 0.3125
Outputs:
- updated: float32 [384, 64, 512], P(None, 'lat', 'lon')
All inputs are finite; a program needn't handle non-finite values.
Results may differ from a plain program's by a relative error of at most 0.0044.
Values may be sent and summed in bfloat16 or wider, within the bound.
A program may use at most 64 MiB of HBM per device.

v0:
```python
import math
import jax
import jax.numpy as jnp
from jax import lax
from jax.sharding import PartitionSpec as P

M_DEV = 8
HALO = 2


def padded_2(cells, sides, width):
    for axis, dim in sides:
        count = lax.axis_size(axis)
        head = lax.slice_in_dim(cells, 0, width, axis=dim)
        tail = lax.slice_in_dim(cells, cells.shape[dim] - width, cells.shape[dim], axis=dim)
        cells = jnp.concatenate(
            [
                lax.ppermute(tail, axis, [(i, (i + 1) % count) for i in range(count)]),
                cells,
                lax.ppermute(head, axis, [((i + 1) % count, i) for i in range(count)]),
            ],
            axis=dim,
        )
    return cells


def legendre_table(first_order, local_orders, all_orders, degrees, nlat):
    lat_pos = jnp.arange(nlat, dtype=jnp.float32)
    colatitude = math.pi * (lat_pos + 0.5) / nlat
    cosine = jnp.cos(colatitude)
    sine = jnp.sin(colatitude)
    counters = jnp.arange(1, all_orders, dtype=jnp.float32)
    cumulative = jnp.concatenate(
        [
            jnp.zeros((1,), jnp.float32),
            jnp.cumsum(jnp.log((2.0 * counters - 1.0) / (2.0 * counters))),
        ]
    )
    log_product = lax.dynamic_slice_in_dim(cumulative, first_order, local_orders)
    orders = first_order + jnp.arange(local_orders, dtype=jnp.int32)
    order_real = orders.astype(jnp.float32)[:, None]
    log_seed = (
        0.5 * (jnp.log((2.0 * order_real + 1.0) / (4.0 * math.pi)) + log_product[:, None])
        + order_real * jnp.log(sine)[None, :]
    )
    rescale = jnp.clip(-log_seed, 0.0, 80.0)
    seed_value = jnp.exp(log_seed + rescale)
    undo = jnp.exp(-rescale)

    def advance(state_pair, degree):
        previous, before_last = state_pair
        degree_real = degree.astype(jnp.float32)
        factor_a = jnp.sqrt(
            jnp.maximum(4.0 * degree_real**2 - 1.0, 1.0)
            / jnp.maximum(degree_real**2 - order_real**2, 1.0)
        )
        factor_b = jnp.sqrt(
            jnp.maximum((degree_real - 1.0) ** 2 - order_real**2, 0.0)
            / jnp.maximum(4.0 * (degree_real - 1.0) ** 2 - 1.0, 1.0)
        )
        recurred = factor_a * (cosine[None, :] * previous - factor_b * before_last)
        current = jnp.where(
            degree == orders[:, None],
            seed_value,
            jnp.where(degree > orders[:, None], recurred, 0.0),
        )
        return ((current, previous), current * undo)

    empty = jnp.zeros((local_orders, nlat), jnp.float32)
    final_pair, table = lax.scan(
        advance, (empty, empty), jnp.arange(degrees, dtype=jnp.int32), unroll=8
    )
    return table


def disco_rows(padded, disco_dlat, disco_dlon, disco_basis, disco_quad, disco_weight, width):
    basis_count = disco_weight.shape[0]
    channels = padded.shape[0]
    zero_index = jnp.zeros((), jnp.int32)

    def one_row(inputs):
        row_index, lat_offsets, lon_offsets, basis_row, quad_row = inputs
        sources = row_index + HALO + lat_offsets
        begins = HALO + lon_offsets

        def take(source, begin):
            return lax.dynamic_slice(padded, (zero_index, source, begin), (channels, 1, width))[
                :, 0, :
            ]

        support = jax.vmap(take)(sources, begins)
        selector = (basis_row[:, None] == jnp.arange(basis_count, dtype=jnp.int32)[None, :]).astype(
            jnp.float32
        ) * quad_row[:, None]
        aggregate = jnp.einsum(
            "kb,kcj->bcj", selector, support, precision=lax.Precision.HIGHEST
        ).astype(jnp.bfloat16)
        return lax.dot_general(
            disco_weight,
            aggregate,
            (((0, 1), (0, 1)), ((), ())),
            preferred_element_type=jnp.float32,
        )

    row_count = disco_dlat.shape[0]
    stacked = lax.map(
        one_row,
        (jnp.arange(row_count, dtype=jnp.int32), disco_dlat, disco_dlon, disco_basis, disco_quad),
    )
    return jnp.transpose(stacked, (1, 0, 2))


def per_device(
    grid_field,
    disco_dlat,
    disco_dlon,
    disco_basis,
    disco_quad,
    disco_weight,
    norm_gain,
    spectral_filter,
    mix_weight,
):
    lat_count = lax.axis_size("lat")
    lon_count = lax.axis_size("lon")
    channels, lat_local, lon_local = grid_field.shape
    lat_total = lat_local * lat_count
    lon_total = lon_local * lon_count
    mode_count = M_DEV * lat_count
    chan_local = channels // lon_count
    lat_index = lax.axis_index("lat")
    lon_index = lax.axis_index("lon")
    wrapped = padded_2(grid_field, (("lat", 1), ("lon", 2)), HALO)
    global_rows = lat_index * lat_local + jnp.arange(lat_local + 2 * HALO, dtype=jnp.int32) - HALO
    inside = (global_rows >= 0) & (global_rows < lat_total)
    padded = jnp.where(inside[None, :, None], wrapped, 0.0)
    after_conv = grid_field + disco_rows(
        padded, disco_dlat, disco_dlon, disco_basis, disco_quad, disco_weight, lon_local
    )
    mean_square = jnp.mean(after_conv * after_conv, axis=0, keepdims=True)
    normed = after_conv * lax.rsqrt(mean_square + 1e-06) * norm_gain[:, None, None]
    lon_pos = jnp.arange(lon_total, dtype=jnp.int32)
    mode_pos = jnp.arange(mode_count, dtype=jnp.int32)
    phase = (lon_pos[:, None] * mode_pos[None, :] % lon_total).astype(jnp.float32) * (
        2.0 * math.pi / lon_total
    )
    cos_part = jnp.cos(phase)
    sin_part = jnp.sin(phase)
    forward_table = jnp.concatenate([cos_part, -sin_part], axis=1) * (2.0 * math.pi / lon_total)
    mode_weight = jnp.where(mode_pos == 0, 1.0, 2.0).astype(jnp.float32)[None, :]
    inverse_table = jnp.transpose(
        jnp.concatenate([cos_part * mode_weight, -sin_part * mode_weight], axis=1)
    )
    portion = lax.all_to_all(normed, "lon", split_axis=0, concat_axis=2, tiled=True)
    result = jnp.einsum("crj,jq->qcr", portion, forward_table, precision=lax.Precision.HIGHEST)
    fourier = result.reshape(2, mode_count, portion.shape[0], portion.shape[1])
    table = legendre_table(lat_index * M_DEV, M_DEV, mode_count, mode_count, lat_total)
    lat_pos = jnp.arange(lat_total, dtype=jnp.float32)
    quad_weight = math.pi / lat_total * jnp.sin(math.pi * (lat_pos + 0.5) / lat_total)
    local_filter = lax.dynamic_slice_in_dim(spectral_filter, lon_index * chan_local, chan_local, 0)
    weighted = lax.all_to_all(fourier, "lat", split_axis=1, concat_axis=3, tiled=True) * quad_weight
    spectra = jnp.einsum("rmck,lmk->rmcl", weighted, table, precision=lax.Precision.HIGHEST)
    filtered = spectra * local_filter[None, None]
    synthesis = jnp.einsum("rmcl,lmk->rmck", filtered, table, precision=lax.Precision.HIGHEST)
    returned = lax.all_to_all(synthesis, "lat", split_axis=3, concat_axis=1, tiled=True)
    wave_field = jnp.einsum(
        "qcr,qj->crj",
        returned.reshape(2 * mode_count, chan_local, lat_local),
        inverse_table,
        precision=lax.Precision.HIGHEST,
    )
    activated_local = jax.nn.gelu(wave_field, approximate=True).astype(jnp.bfloat16)
    activated = lax.all_to_all(activated_local, "lon", split_axis=2, concat_axis=0, tiled=True)
    mixed = lax.dot_general(
        mix_weight, activated, (((0,), (0,)), ((), ())), preferred_element_type=jnp.float32
    )
    return after_conv + mixed


def solution(mesh):
    placed = (
        P(None, "lat", "lon"),
        P("lat", None),
        P("lat", None),
        P("lat", None),
        P("lat", None),
        P(),
        P(),
        P(),
        P(),
    )
    return jax.shard_map(
        per_device, mesh=mesh, in_specs=placed, out_specs=P(None, "lat", "lon"), check_vma=False
    )
```

profile of v0, /device:TPU:0, one launch (start us, length us, event | category | flops | bytes accessed | tf_op | source)
XLA Modules:
  0.0 368.7 jit_solution(16414946515964665758)
XLA Ops:
  9.4 14.1 %collective-permute-done = f32[384,2,128]{0,1,2:T(2,128)} collective-permute-done((f32[384,2,128]{0,1,2:T(2,128)}, f32[384,2,128]{0,1,2:T(2,128)}, u32[]{:S(2)}, u32[]{:S(2)}) %collective-permute-start) | collective-permute-done | bytes 393248 | tf_op jit(solution)/shard_map/ppermute | solution.py:18
  32.9 146.3 %while.33 = (s32[]{:T(128)}, f32[8,384,128]{1,2,0:T(8,128)}, s32[8,16]{1,0:T(8,128)}, f32[8,16]{1,0:T(8,128)}, s32[8]{0:T(128)S(1)}, /*index=5*/s32[8,16]{1,0:T(...) while((s32[]{:T(128)}, f32[8,384,128]{1,2,0:T(8,128)}, ...), condition=%wide.region_1.2_spmd, body=%wide.region_0.1_spmd.sunk | while | flops 188940624 | bytes 22611376 | solution.py:106
  35.0 6.6 %gather_fusion = f32[16,384,128]{1,0,2:T(8,128)} fusion(f32[384,12,132]{0,1,2:T(8,128)S(1)} %get-tuple-element.853, s32[16]{0:T(128)S(1)} %or_bitcast_fusion.2), kind=kCustom, calls=%fused_computation.clone.1 | custom fusion | bytes 6291648 | tf_op jit(solution)/shard_map/while/body/eval_jaxpr/vmap()/gather | solution.py:87
  41.5 3.6 copy.119
  53.3 6.6 %gather_fusion = f32[16,384,128]{1,0,2:T(8,128)} fusion(f32[384,12,132]{0,1,2:T(8,128)S(1)} %get-tuple-element.853, s32[16]{0:T(128)S(1)} %or_bitcast_fusion.2), kind=kCustom, calls=%fused_computation.clone.1 | custom fusion | bytes 6291648 | tf_op jit(solution)/shard_map/while/body/eval_jaxpr/vmap()/gather | solution.py:87
  59.8 3.6 copy.119
  71.6 6.6 %gather_fusion = f32[16,384,128]{1,0,2:T(8,128)} fusion(f32[384,12,132]{0,1,2:T(8,128)S(1)} %get-tuple-element.853, s32[16]{0:T(128)S(1)} %or_bitcast_fusion.2), kind=kCustom, calls=%fused_computation.clone.1 | custom fusion | bytes 6291648 | tf_op jit(solution)/shard_map/while/body/eval_jaxpr/vmap()/gather | solution.py:87
  78.1 3.6 copy.119
  89.8 6.6 %gather_fusion = f32[16,384,128]{1,0,2:T(8,128)} fusion(f32[384,12,132]{0,1,2:T(8,128)S(1)} %get-tuple-element.853, s32[16]{0:T(128)S(1)} %or_bitcast_fusion.2), kind=kCustom, calls=%fused_computation.clone.1 | custom fusion | bytes 6291648 | tf_op jit(solution)/shard_map/while/body/eval_jaxpr/vmap()/gather | solution.py:87
  96.4 3.6 copy.119
  108.1 6.6 %gather_fusion = f32[16,384,128]{1,0,2:T(8,128)} fusion(f32[384,12,132]{0,1,2:T(8,128)S(1)} %get-tuple-element.853, s32[16]{0:T(128)S(1)} %or_bitcast_fusion.2), kind=kCustom, calls=%fused_computation.clone.1 | custom fusion | bytes 6291648 | tf_op jit(solution)/shard_map/while/body/eval_jaxpr/vmap()/gather | solution.py:87
  126.4 6.6 %gather_fusion = f32[16,384,128]{1,0,2:T(8,128)} fusion(f32[384,12,132]{0,1,2:T(8,128)S(1)} %get-tuple-element.853, s32[16]{0:T(128)S(1)} %or_bitcast_fusion.2), kind=kCustom, calls=%fused_computation.clone.1 | custom fusion | bytes 6291648 | tf_op jit(solution)/shard_map/while/body/eval_jaxpr/vmap()/gather | solution.py:87
  132.9 3.6 copy.119
  144.7 6.6 %gather_fusion = f32[16,384,128]{1,0,2:T(8,128)} fusion(f32[384,12,132]{0,1,2:T(8,128)S(1)} %get-tuple-element.853, s32[16]{0:T(128)S(1)} %or_bitcast_fusion.2), kind=kCustom, calls=%fused_computation.clone.1 | custom fusion | bytes 6291648 | tf_op jit(solution)/shard_map/while/body/eval_jaxpr/vmap()/gather | solution.py:87
  151.2 3.6 copy.119
  162.9 6.6 %gather_fusion = f32[16,384,128]{1,0,2:T(8,128)} fusion(f32[384,12,132]{0,1,2:T(8,128)S(1)} %get-tuple-element.853, s32[16]{0:T(128)S(1)} %or_bitcast_fusion.2), kind=kCustom, calls=%fused_computation.clone.1 | custom fusion | bytes 6291648 | tf_op jit(solution)/shard_map/while/body/eval_jaxpr/vmap()/gather | solution.py:87
  169.5 3.6 copy.119
  184.9 3.7 %all-to-all-start = ((f32[384,8,128]{2,1,0:T(8,128)}), f32[384,8,128]{2,1,0:T(8,128)S(1)}, u32[]{:S(2)}, u32[]{:S(2)}) async-start(f32[384,8,128]{2,1,0:T(8,128)} %copy.83), calls=%async_computation | async-start | bytes 3145728 | tf_op jit(solution)/shard_map/all_to_all | solution.py:154
  192.8 15.7 %all-to-all-done = f32[384,8,128]{2,1,0:T(8,128)S(1)} async-done(((f32[384,8,128]{2,1,0:T(8,128)}), f32[384,8,128]{2,1,0:T(8,128)S(1)}, u32[]{:S(2)}, u32[]{:S(2)}) %all-to-all-start) | async-done | bytes 1572896 | tf_op jit(solution)/shard_map/all_to_all | solution.py:154
  216.6 4.6 %all-to-all-start.1 = ((f32[2,64,96,8]{2,3,0,1:T(8,128)}), f32[2,64,96,8]{2,3,0,1:T(8,128)S(1)}, u32[]{:S(2)}, u32[]{:S(2)}) async-start(f32[2,64,96,8]{2,3,0,1:T(8,128)} %copy.85), calls=%async_computation.1 | async-start | bytes 1048576 | tf_op jit(solution)/shard_map/all_to_all | solution.py:161
  221.3 95.3 %while.34 = (s32[]{:T(128)}, f32[8,64]{1,0:T(8,128)S(1)}, f32[8,64]{1,0:T(8,128)S(1)}, f32[8,8,8,64]{3,2,1,0:T(8,128)S(1)}, s32[8,8]{1,0:T(8,128)S(1)}, /*index=...) while((s32[]{:T(128)}, f32[8,64]{1,0:T(8,128)S(1)}, ...), condition=%wide.region_4.5_spmd.clone.clone.clone.clone, body=%wide.region_3.4_spmd.clone.clone.clone.clone.sunk | while | flops 93138 | bytes 238507 | solution.py:70
  320.2 6.0 %all-to-all-start.2 = ((f32[2,8,96,64]{2,0,1,3:T(2,128)}), f32[2,8,96,64]{2,0,1,3:T(2,128)S(1)}, u32[]{:S(2)}, u32[]{:S(2)}) async-start(f32[2,8,96,64]{2,0,1,3:T(2,128)} %copy.91), calls=%async_computation.2 | async-start | bytes 1048576 | tf_op jit(solution)/shard_map/all_to_all | solution.py:165
  327.3 12.6 %all-to-all-done.2 = f32[2,8,96,64]{2,0,1,3:T(2,128)S(1)} async-done(((f32[2,8,96,64]{2,0,1,3:T(2,128)}), f32[2,8,96,64]{2,0,1,3:T(2,128)S(1)}, u32[]{:S(2)}, u32[]{:S(2)}) %all-to-all-start.2) | async-done | bytes 393248 | tf_op jit(solution)/shard_map/all_to_all | solution.py:165
  345.2 17.6 %all_to_all.69 = bf16[96,8,512]{0,1,2:T(8,128)(2,1)} all-to-all(bf16[96,8,512]{0,1,2:T(8,128)(2,1)S(1)} %copy.94), channel_id=1, replica_groups=mesh['lat'=8,'lon'=4] {'lon'}, dimensions={2} | all-to-all | bytes 1572864 | tf_op jit(solution)/shard_map/all_to_all | solution.py:173
  (357 shorter events, 168.8 us)
Async XLA Ops:
  0.0 365.0 %copy-start = (bf16[384,384]{1,0:T(8,128)(2,1)S(1)}, bf16[384,384]{1,0:T(8,128)(2,1)}, u32[]{:S(2)}) copy-start(bf16[384,384]{1,0:T(8,128)(2,1)} %param.21) | copy-start | bytes 884740
  2.0 24.4 %copy-start.3 = (f32[384,8,128]{0,1,2:T(8,128)}, f32[384,8,128]{0,1,2:T(8,128)S(1)}, u32[]{:S(2)}) copy-start(f32[384,8,128]{0,1,2:T(8,128)S(1)} %copy.78) | copy-start | bytes 4718596
  3.3 24.9 %copy-start.4 = (f32[384,8,128]{2,1,0:T(8,128)S(1)}, f32[384,8,128]{2,1,0:T(8,128)}, u32[]{:S(2)}) copy-start(f32[384,8,128]{2,1,0:T(8,128)} %param.13) | copy-start | bytes 4718596
  3.3 20.1 %collective-permute-start = (f32[384,2,128]{0,1,2:T(2,128)}, f32[384,2,128]{0,1,2:T(2,128)}, u32[]{:S(2)}, u32[]{:S(2)}) collective-permute-start(f32[384,2,128]{0,1,2:T(2,128)} %get-tuple-element.570), channel_id=1, source_target_pairs={{0,4},{4,8},{8,12},{12,16},{16,20},{20,24},{24,28},{28,0},{1,5},{5... | collective-permute-start | bytes 1179656 | tf_op jit(solution)/shard_map/ppermute | solution.py:18
  6.3 19.3 %collective-permute-start.1 = (f32[384,2,128]{0,1,2:T(2,128)}, f32[384,2,128]{0,1,2:T(2,128)}, u32[]{:S(2)}, u32[]{:S(2)}) collective-permute-start(f32[384,2,128]{0,1,2:T(2,128)} %get-tuple-element.571), channel_id=1, source_target_pairs={{4,0},{8,4},{12,8},{16,12},{20,16},{24,20},{28,24},{0,28},{5,1},{9... | collective-permute-start | bytes 1179656 | tf_op jit(solution)/shard_map/ppermute | solution.py:20
  26.4 3.6 collective-permute-start.2
  26.5 4.1 %collective-permute-start.3 = (f32[384,12,2]{0,1,2:T(8,128)S(1)}, f32[384,12,2]{0,1,2:T(8,128)}, u32[]{:S(2)}, u32[]{:S(2)}) collective-permute-start(f32[384,12,2]{0,1,2:T(8,128)S(1)} %get-tuple-element.569), channel_id=1, source_target_pairs={{1,0},{2,1},{3,2},{0,3},{5,4},{6,5},{7,6},{4,7},{9,8},{10,9},{11,1... | collective-permute-start | bytes 110600 | tf_op jit(solution)/shard_map/ppermute | solution.py:20
  30.0 0.6 copy-start.6
  46.5 3.6 copy-start.1
  64.8 3.6 copy-start.1
  83.1 3.6 copy-start.1
  101.4 3.6 copy-start.1
  119.7 3.6 copy-start.1
  137.9 3.6 copy-start.1
  156.2 3.6 copy-start.1
  174.5 3.6 copy-start.1
  179.2 2.4 copy-start.2
  179.2 2.4 copy-start.7
  184.9 23.6 %all-to-all-start = ((f32[384,8,128]{2,1,0:T(8,128)}), f32[384,8,128]{2,1,0:T(8,128)S(1)}, u32[]{:S(2)}, u32[]{:S(2)}) async-start(f32[384,8,128]{2,1,0:T(8,128)} %copy.83), calls=%async_computation | async-start | bytes 3145728 | tf_op jit(solution)/shard_map/all_to_all | solution.py:154
  215.5 5.7 %copy-start.5 = (f32[8,8,8,64]{3,2,1,0:T(8,128)S(1)}, f32[8,8,8,64]{3,2,1,0:T(8,128)}, u32[]{:S(2)}) copy-start(f32[8,8,8,64]{3,2,1,0:T(8,128)} %custom-call.6) | copy-start | bytes 393220
  216.6 101.1 %all-to-all-start.1 = ((f32[2,64,96,8]{2,3,0,1:T(8,128)}), f32[2,64,96,8]{2,3,0,1:T(8,128)S(1)}, u32[]{:S(2)}, u32[]{:S(2)}) async-start(f32[2,64,96,8]{2,3,0,1:T(8,128)} %copy.85), calls=%async_computation.1 | async-start | bytes 1048576 | tf_op jit(solution)/shard_map/all_to_all | solution.py:161
  320.2 19.7 %all-to-all-start.2 = ((f32[2,8,96,64]{2,0,1,3:T(2,128)}), f32[2,8,96,64]{2,0,1,3:T(2,128)S(1)}, u32[]{:S(2)}, u32[]{:S(2)}) async-start(f32[2,8,96,64]{2,0,1,3:T(2,128)} %copy.91), calls=%async_computation.2 | async-start | bytes 1048576 | tf_op jit(solution)/shard_map/all_to_all | solution.py:165
where the time goes:
time: 371 us; the launch traced here: 369 us
  local copies, waits for them, and re-layouts  126 us (34%)
  other arithmetic  63.9 us (17%)
  loops' own time  47.8 us (13%)
  matrix products  46.6 us (13%)
  waiting for transfers between devices  44.6 us (12%)
  starting transfers between devices  22.2 us (6%)
  blocking collectives  17.6 us (5%)
    gather x16, local copies, waits for them, and re-layouts, take(): lax.dynamic_slice(padded, (zero_index, source, begin), (channels, 1, width))  81.2 us
    another operation x1, loops' own time, legendre_table(): lax.scan(advance, (empty, empty), jnp.arange(degrees, dtype=jnp.int32), u...  42.2 us
    gt x64, other arithmetic, advance(): degree > orders[:, None]  40.5 us
    dot_general x8, matrix products, one_row(): jnp.einsum('kb,kcj->bcj', selector, support, precision=lax.Precision.HIGH...  28.7 us
    all_to_all x1, blocking collectives, per_device(): lax.all_to_all(activated_local, 'lon', split_axis=2, concat_axis=0, tiled...  17.6 us
    all_to_all x1, waiting for transfers between devices, per_device(): lax.all_to_all(normed, 'lon', split_axis=0, concat_axis=2, tiled=True)  15.7 us
    ppermute x2, waiting for transfers between devices, padded_2(): lax.ppermute(tail, axis, [(i, (i + 1) % count) for i in range(count)])  14.1 us
    all_to_all x1, waiting for transfers between devices, per_device(): lax.all_to_all(synthesis, 'lat', split_axis=3, concat_axis=1, tiled=True)  12.6 us
  transfers between devices with their start and end apart: 7, of which 5 were waited for; matrix products, arithmetic and copies ran while one was open for 17% of the time, Pallas kernels for 0%

commit v1 on v0

--- a/solution.py
+++ b/solution.py
@@ -6,6 +6,28 @@
 
 M_DEV = 8
 HALO = 2
+
+
+def cut_along(x, dim, devices):
+    before, after = (x.shape[:dim], x.shape[dim + 1 :])
+    return jnp.moveaxis(x.reshape(*before, devices, -1, *after), dim, 0)
+
+
+def joined_along(tiles, dim):
+    tiles = jnp.moveaxis(tiles, 0, dim)
+    shape = tiles.shape
+    return tiles.reshape(*shape[:dim], shape[dim] * shape[dim + 1], *shape[dim + 2 :])
+
+
+def exchange_in_pairs(shard, axis, split_dim, concat_dim):
+    size, index = (lax.axis_size(axis), lax.axis_index(axis))
+    tiles = cut_along(shard, split_dim, size)
+    outs = [tiles[index]]
+    for step in range(1, size):
+        sent = tiles[index ^ step]
+        outs.append(lax.ppermute(sent, axis, [(i, i ^ step) for i in range(size)]))
+    tiles = jnp.stack(outs)[index ^ jnp.arange(size)]
+    return joined_along(tiles, concat_dim)
 
 
 def padded_2(cells, sides, width):
@@ -170,7 +192,7 @@
         precision=lax.Precision.HIGHEST,
     )
     activated_local = jax.nn.gelu(wave_field, approximate=True).astype(jnp.bfloat16)
-    activated = lax.all_to_all(activated_local, "lon", split_axis=2, concat_axis=0, tiled=True)
+    activated = exchange_in_pairs(activated_local, "lon", 2, 0)
     mixed = lax.dot_general(
         mix_weight, activated, (((0,), (0,)), ((), ())), preferred_element_type=jnp.float32
     )

time: 371 us -> 360 us (0.970)
  blocking collectives: 17.6 us -> 0 us
  waiting for transfers between devices: 44.6 us -> 53.7 us
    all_to_all x1 -> x0, blocking collectives: 17.6 us -> none  [per_device(): lax.all_to_all(activated_local, 'lon', split_axis=2, concat_axis=0, tiled...]
    ppermute x0 -> x3, waiting for transfers between devices: none -> 9.1 us  [exchange_in_pairs(): outs.append(lax.ppermute(sent, axis, [(i, i ^ step) for i in range(size)]))]
  transfers between devices with their start and end apart: 7 -> 10, of which waited for: 5 -> 7; matrix products, arithmetic and copies ran while one was open for 17% -> 17% of each run, Pallas kernels for 0% -> 0%
where the time goes in v1:
time: 360 us; the launch traced here: 357 us
  local copies, waits for them, and re-layouts  123 us (34%)
  other arithmetic  63.4 us (18%)
  waiting for transfers between devices  53.7 us (15%)
  loops' own time  46.8 us (13%)
  matrix products  46 us (13%)
  starting transfers between devices  24.1 us (7%)
    gather x16, local copies, waits for them, and re-layouts, take(): lax.dynamic_slice(padded, (zero_index, source, begin), (channels, 1, width))  81.1 us
    another operation x1, loops' own time, legendre_table(): lax.scan(advance, (empty, empty), jnp.arange(degrees, dtype=jnp.int32), u...  41.6 us
    gt x64, other arithmetic, advance(): degree > orders[:, None]  39.9 us
    dot_general x8, matrix products, one_row(): jnp.einsum('kb,kcj->bcj', selector, support, precision=lax.Precision.HIGH...  28.7 us
    all_to_all x1, waiting for transfers between devices, per_device(): lax.all_to_all(normed, 'lon', split_axis=0, concat_axis=2, tiled=True)  15.7 us
    ppermute x2, waiting for transfers between devices, padded_2(): lax.ppermute(tail, axis, [(i, (i + 1) % count) for i in range(count)])  14.1 us
    all_to_all x1, waiting for transfers between devices, per_device(): lax.all_to_all(synthesis, 'lat', split_axis=3, concat_axis=1, tiled=True)  12.6 us
    ppermute x3, waiting for transfers between devices, exchange_in_pairs(): outs.append(lax.ppermute(sent, axis, [(i, i ^ step) for i in range(size)]))  9.1 us
  transfers between devices with their start and end apart: 10, of which 7 were waited for; matrix products, arithmetic and copies ran while one was open for 17% of the time, Pallas kernels for 0%

profile of v1, /device:TPU:0, one launch (start us, length us, event | category | flops | bytes accessed | tf_op | source)
XLA Modules:
  0.0 357.5 jit_solution(3303219388491454175)
XLA Ops:
  9.4 14.1 %collective-permute-done = f32[384,2,128]{0,1,2:T(2,128)} collective-permute-done((f32[384,2,128]{0,1,2:T(2,128)}, f32[384,2,128]{0,1,2:T(2,128)}, u32[]{:S(2)}, u32[]{:S(2)}) %collective-permute-start) | collective-permute-done | bytes 393248 | tf_op jit(solution)/shard_map/ppermute | solution.py:40
  32.9 145.7 %while.33 = (s32[]{:T(128)}, f32[8,384,128]{1,2,0:T(8,128)}, s32[8,16]{1,0:T(8,128)}, f32[8,16]{1,0:T(8,128)}, s32[8]{0:T(128)S(1)}, /*index=5*/s32[8,16]{1,0:T(...) while((s32[]{:T(128)}, f32[8,384,128]{1,2,0:T(8,128)}, ...), condition=%wide.region_1.2_spmd, body=%wide.region_0.1_spmd.sunk | while | flops 188940624 | bytes 22611376 | solution.py:128
  34.9 6.5 %gather_fusion = f32[16,384,128]{1,0,2:T(8,128)} fusion(f32[384,12,132]{0,1,2:T(8,128)S(1)} %get-tuple-element.857, s32[16]{0:T(128)S(1)} %or_bitcast_fusion.2), kind=kCustom, calls=%fused_computation.clone.1 | custom fusion | bytes 6291648 | tf_op jit(solution)/shard_map/while/body/eval_jaxpr/vmap()/gather | solution.py:109
  41.5 3.6 %copy.90 = f32[16,384,128]{2,0,1:T(8,128)} copy(f32[16,384,128]{1,0,2:T(8,128)} %gather_fusion) | data formatting | bytes 6291456 | tf_op jit(solution)/shard_map/while/body/eval_jaxpr/vmap()/gather | solution.py:109
  53.2 6.5 %gather_fusion = f32[16,384,128]{1,0,2:T(8,128)} fusion(f32[384,12,132]{0,1,2:T(8,128)S(1)} %get-tuple-element.857, s32[16]{0:T(128)S(1)} %or_bitcast_fusion.2), kind=kCustom, calls=%fused_computation.clone.1 | custom fusion | bytes 6291648 | tf_op jit(solution)/shard_map/while/body/eval_jaxpr/vmap()/gather | solution.py:109
  59.7 3.6 %copy.90 = f32[16,384,128]{2,0,1:T(8,128)} copy(f32[16,384,128]{1,0,2:T(8,128)} %gather_fusion) | data formatting | bytes 6291456 | tf_op jit(solution)/shard_map/while/body/eval_jaxpr/vmap()/gather | solution.py:109
  71.4 6.5 %gather_fusion = f32[16,384,128]{1,0,2:T(8,128)} fusion(f32[384,12,132]{0,1,2:T(8,128)S(1)} %get-tuple-element.857, s32[16]{0:T(128)S(1)} %or_bitcast_fusion.2), kind=kCustom, calls=%fused_computation.clone.1 | custom fusion | bytes 6291648 | tf_op jit(solution)/shard_map/while/body/eval_jaxpr/vmap()/gather | solution.py:109
  77.9 3.6 %copy.90 = f32[16,384,128]{2,0,1:T(8,128)} copy(f32[16,384,128]{1,0,2:T(8,128)} %gather_fusion) | data formatting | bytes 6291456 | tf_op jit(solution)/shard_map/while/body/eval_jaxpr/vmap()/gather | solution.py:109
  89.6 6.5 %gather_fusion = f32[16,384,128]{1,0,2:T(8,128)} fusion(f32[384,12,132]{0,1,2:T(8,128)S(1)} %get-tuple-element.857, s32[16]{0:T(128)S(1)} %or_bitcast_fusion.2), kind=kCustom, calls=%fused_computation.clone.1 | custom fusion | bytes 6291648 | tf_op jit(solution)/shard_map/while/body/eval_jaxpr/vmap()/gather | solution.py:109
  96.1 3.6 %copy.90 = f32[16,384,128]{2,0,1:T(8,128)} copy(f32[16,384,128]{1,0,2:T(8,128)} %gather_fusion) | data formatting | bytes 6291456 | tf_op jit(solution)/shard_map/while/body/eval_jaxpr/vmap()/gather | solution.py:109
  107.8 6.5 %gather_fusion = f32[16,384,128]{1,0,2:T(8,128)} fusion(f32[384,12,132]{0,1,2:T(8,128)S(1)} %get-tuple-element.857, s32[16]{0:T(128)S(1)} %or_bitcast_fusion.2), kind=kCustom, calls=%fused_computation.clone.1 | custom fusion | bytes 6291648 | tf_op jit(solution)/shard_map/while/body/eval_jaxpr/vmap()/gather | solution.py:109
  114.3 3.6 %copy.90 = f32[16,384,128]{2,0,1:T(8,128)} copy(f32[16,384,128]{1,0,2:T(8,128)} %gather_fusion) | data formatting | bytes 6291456 | tf_op jit(solution)/shard_map/while/body/eval_jaxpr/vmap()/gather | solution.py:109
  126.0 6.5 %gather_fusion = f32[16,384,128]{1,0,2:T(8,128)} fusion(f32[384,12,132]{0,1,2:T(8,128)S(1)} %get-tuple-element.857, s32[16]{0:T(128)S(1)} %or_bitcast_fusion.2), kind=kCustom, calls=%fused_computation.clone.1 | custom fusion | bytes 6291648 | tf_op jit(solution)/shard_map/while/body/eval_jaxpr/vmap()/gather | solution.py:109
  132.5 3.6 %copy.90 = f32[16,384,128]{2,0,1:T(8,128)} copy(f32[16,384,128]{1,0,2:T(8,128)} %gather_fusion) | data formatting | bytes 6291456 | tf_op jit(solution)/shard_map/while/body/eval_jaxpr/vmap()/gather | solution.py:109
  144.2 6.5 %gather_fusion = f32[16,384,128]{1,0,2:T(8,128)} fusion(f32[384,12,132]{0,1,2:T(8,128)S(1)} %get-tuple-element.857, s32[16]{0:T(128)S(1)} %or_bitcast_fusion.2), kind=kCustom, calls=%fused_computation.clone.1 | custom fusion | bytes 6291648 | tf_op jit(solution)/shard_map/while/body/eval_jaxpr/vmap()/gather | solution.py:109
  150.7 3.6 %copy.90 = f32[16,384,128]{2,0,1:T(8,128)} copy(f32[16,384,128]{1,0,2:T(8,128)} %gather_fusion) | data formatting | bytes 6291456 | tf_op jit(solution)/shard_map/while/body/eval_jaxpr/vmap()/gather | solution.py:109
  162.4 6.5 %gather_fusion = f32[16,384,128]{1,0,2:T(8,128)} fusion(f32[384,12,132]{0,1,2:T(8,128)S(1)} %get-tuple-element.857, s32[16]{0:T(128)S(1)} %or_bitcast_fusion.2), kind=kCustom, calls=%fused_computation.clone.1 | custom fusion | bytes 6291648 | tf_op jit(solution)/shard_map/while/body/eval_jaxpr/vmap()/gather | solution.py:109
  184.3 3.7 %all-to-all-start = ((f32[384,8,128]{2,1,0:T(8,128)}), f32[384,8,128]{2,1,0:T(8,128)S(1)}, u32[]{:S(2)}, u32[]{:S(2)}) async-start(f32[384,8,128]{2,1,0:T(8,128)} %copy.57), calls=%async_computation | async-start | bytes 3145728 | tf_op jit(solution)/shard_map/all_to_all | solution.py:176
  192.2 15.7 %all-to-all-done = f32[384,8,128]{2,1,0:T(8,128)S(1)} async-done(((f32[384,8,128]{2,1,0:T(8,128)}), f32[384,8,128]{2,1,0:T(8,128)S(1)}, u32[]{:S(2)}, u32[]{:S(2)}) %all-to-all-start) | async-done | bytes 1572896 | tf_op jit(solution)/shard_map/all_to_all | solution.py:176
  216.1 4.6 %all-to-all-start.1 = ((f32[2,64,96,8]{2,3,0,1:T(8,128)}), f32[2,64,96,8]{2,3,0,1:T(8,128)S(1)}, u32[]{:S(2)}, u32[]{:S(2)}) async-start(f32[2,64,96,8]{2,3,0,1:T(8,128)} %copy.59), calls=%async_computation.1 | async-start | bytes 1048576 | tf_op jit(solution)/shard_map/all_to_all | solution.py:183
  220.7 94.3 %while.34 = (s32[]{:T(128)}, f32[8,64]{1,0:T(8,128)S(1)}, f32[8,64]{1,0:T(8,128)S(1)}, f32[8,8,8,64]{3,2,1,0:T(8,128)S(1)}, s32[8,8]{1,0:T(8,128)S(1)}, /*index=...) while((s32[]{:T(128)}, f32[8,64]{1,0:T(8,128)S(1)}, ...), condition=%wide.region_4.5_spmd.clone.clone.clone.clone, body=%wide.region_3.4_spmd.clone.clone.clone.clone.sunk | while | flops 93138 | bytes 238507 | solution.py:92
  318.6 6.0 %all-to-all-start.2 = ((f32[2,8,96,64]{2,0,1,3:T(2,128)}), f32[2,8,96,64]{2,0,1,3:T(2,128)S(1)}, u32[]{:S(2)}, u32[]{:S(2)}) async-start(f32[2,8,96,64]{2,0,1,3:T(2,128)} %copy.65), calls=%async_computation.2 | async-start | bytes 1048576 | tf_op jit(solution)/shard_map/all_to_all | solution.py:187
  325.7 12.6 %all-to-all-done.2 = f32[2,8,96,64]{2,0,1,3:T(2,128)S(1)} async-done(((f32[2,8,96,64]{2,0,1,3:T(2,128)}), f32[2,8,96,64]{2,0,1,3:T(2,128)S(1)}, u32[]{:S(2)}, u32[]{:S(2)}) %all-to-all-start.2) | async-done | bytes 393248 | tf_op jit(solution)/shard_map/all_to_all | solution.py:187
  342.7 6.0 %collective-permute-done.5 = bf16[96,8,128]{2,1,0:T(8,128)(2,1)S(1)} collective-permute-done((bf16[96,8,128]{2,1,0:T(8,128)(2,1)S(1)}, bf16[96,8,128]{2,1,0:T(8,128)(2,1)S(1)}, u32[]{:S(2)}, u32[]{:S(2)}) %collective-permute-start.5) | collective-permute-done | bytes 196640 | tf_op jit(solution)/shard_map/ppermute | solution.py:28
  (364 shorter events, 170.2 us)
Async XLA Ops:
  0.0 353.5 %copy-start = (bf16[384,384]{1,0:T(8,128)(2,1)S(1)}, bf16[384,384]{1,0:T(8,128)(2,1)}, u32[]{:S(2)}) copy-start(bf16[384,384]{1,0:T(8,128)(2,1)} %param.21) | copy-start | bytes 884740
  2.0 24.4 %copy-start.3 = (f32[384,8,128]{0,1,2:T(8,128)}, f32[384,8,128]{0,1,2:T(8,128)S(1)}, u32[]{:S(2)}) copy-start(f32[384,8,128]{0,1,2:T(8,128)S(1)} %copy.52) | copy-start | bytes 4718596
  3.4 24.9 %copy-start.4 = (f32[384,8,128]{2,1,0:T(8,128)S(1)}, f32[384,8,128]{2,1,0:T(8,128)}, u32[]{:S(2)}) copy-start(f32[384,8,128]{2,1,0:T(8,128)} %param.13) | copy-start | bytes 4718596
  3.4 20.1 %collective-permute-start = (f32[384,2,128]{0,1,2:T(2,128)}, f32[384,2,128]{0,1,2:T(2,128)}, u32[]{:S(2)}, u32[]{:S(2)}) collective-permute-start(f32[384,2,128]{0,1,2:T(2,128)} %get-tuple-element.570), channel_id=1, source_target_pairs={{0,4},{4,8},{8,12},{12,16},{16,20},{20,24},{24,28},{28,0},{1,5},{5... | collective-permute-start | bytes 1179656 | tf_op jit(solution)/shard_map/ppermute | solution.py:40
  6.4 19.3 %collective-permute-start.1 = (f32[384,2,128]{0,1,2:T(2,128)}, f32[384,2,128]{0,1,2:T(2,128)}, u32[]{:S(2)}, u32[]{:S(2)}) collective-permute-start(f32[384,2,128]{0,1,2:T(2,128)} %get-tuple-element.571), channel_id=1, source_target_pairs={{4,0},{8,4},{12,8},{16,12},{20,16},{24,20},{28,24},{0,28},{5,1},{9... | collective-permute-start | bytes 1179656 | tf_op jit(solution)/shard_map/ppermute | solution.py:42
  26.5 3.6 collective-permute-start.2
  26.5 4.1 %collective-permute-start.3 = (f32[384,12,2]{0,1,2:T(8,128)S(1)}, f32[384,12,2]{0,1,2:T(8,128)}, u32[]{:S(2)}, u32[]{:S(2)}) collective-permute-start(f32[384,12,2]{0,1,2:T(8,128)S(1)} %get-tuple-element.569), channel_id=1, source_target_pairs={{1,0},{2,1},{3,2},{0,3},{5,4},{6,5},{7,6},{4,7},{9,8},{10,9},{11,1... | collective-permute-start | bytes 110600 | tf_op jit(solution)/shard_map/ppermute | solution.py:42
  46.5 3.6 %copy-start.1 = (bf16[4,384,384]{2,1,0:T(8,128)(2,1)S(1)}, bf16[4,384,384]{2,1,0:T(8,128)(2,1)}, u32[]{:S(2)}) copy-start(bf16[4,384,384]{2,1,0:T(8,128)(2,1)} %get-tuple-element.858) | copy-start | bytes 3538948 | tf_op jit(solution)/shard_map/while
  64.7 3.6 %copy-start.1 = (bf16[4,384,384]{2,1,0:T(8,128)(2,1)S(1)}, bf16[4,384,384]{2,1,0:T(8,128)(2,1)}, u32[]{:S(2)}) copy-start(bf16[4,384,384]{2,1,0:T(8,128)(2,1)} %get-tuple-element.858) | copy-start | bytes 3538948 | tf_op jit(solution)/shard_map/while
  82.9 3.6 %copy-start.1 = (bf16[4,384,384]{2,1,0:T(8,128)(2,1)S(1)}, bf16[4,384,384]{2,1,0:T(8,128)(2,1)}, u32[]{:S(2)}) copy-start(bf16[4,384,384]{2,1,0:T(8,128)(2,1)} %get-tuple-element.858) | copy-start | bytes 3538948 | tf_op jit(solution)/shard_map/while
  101.1 3.6 %copy-start.1 = (bf16[4,384,384]{2,1,0:T(8,128)(2,1)S(1)}, bf16[4,384,384]{2,1,0:T(8,128)(2,1)}, u32[]{:S(2)}) copy-start(bf16[4,384,384]{2,1,0:T(8,128)(2,1)} %get-tuple-element.858) | copy-start | bytes 3538948 | tf_op jit(solution)/shard_map/while
  119.3 3.6 %copy-start.1 = (bf16[4,384,384]{2,1,0:T(8,128)(2,1)S(1)}, bf16[4,384,384]{2,1,0:T(8,128)(2,1)}, u32[]{:S(2)}) copy-start(bf16[4,384,384]{2,1,0:T(8,128)(2,1)} %get-tuple-element.858) | copy-start | bytes 3538948 | tf_op jit(solution)/shard_map/while
  137.5 3.6 %copy-start.1 = (bf16[4,384,384]{2,1,0:T(8,128)(2,1)S(1)}, bf16[4,384,384]{2,1,0:T(8,128)(2,1)}, u32[]{:S(2)}) copy-start(bf16[4,384,384]{2,1,0:T(8,128)(2,1)} %get-tuple-element.858) | copy-start | bytes 3538948 | tf_op jit(solution)/shard_map/while
  155.7 3.6 %copy-start.1 = (bf16[4,384,384]{2,1,0:T(8,128)(2,1)S(1)}, bf16[4,384,384]{2,1,0:T(8,128)(2,1)}, u32[]{:S(2)}) copy-start(bf16[4,384,384]{2,1,0:T(8,128)(2,1)} %get-tuple-element.858) | copy-start | bytes 3538948 | tf_op jit(solution)/shard_map/while
  173.9 3.6 %copy-start.1 = (bf16[4,384,384]{2,1,0:T(8,128)(2,1)S(1)}, bf16[4,384,384]{2,1,0:T(8,128)(2,1)}, u32[]{:S(2)}) copy-start(bf16[4,384,384]{2,1,0:T(8,128)(2,1)} %get-tuple-element.858) | copy-start | bytes 3538948 | tf_op jit(solution)/shard_map/while
  178.7 2.4 copy-start.2
  178.7 2.4 copy-start.7
  184.3 23.6 %all-to-all-start = ((f32[384,8,128]{2,1,0:T(8,128)}), f32[384,8,128]{2,1,0:T(8,128)S(1)}, u32[]{:S(2)}, u32[]{:S(2)}) async-start(f32[384,8,128]{2,1,0:T(8,128)} %copy.57), calls=%async_computation | async-start | bytes 3145728 | tf_op jit(solution)/shard_map/all_to_all | solution.py:176
  215.0 5.7 %copy-start.5 = (f32[8,8,8,64]{3,2,1,0:T(8,128)S(1)}, f32[8,8,8,64]{3,2,1,0:T(8,128)}, u32[]{:S(2)}) copy-start(f32[8,8,8,64]{3,2,1,0:T(8,128)} %custom-call.8) | copy-start | bytes 393220
  216.1 100.1 %all-to-all-start.1 = ((f32[2,64,96,8]{2,3,0,1:T(8,128)}), f32[2,64,96,8]{2,3,0,1:T(8,128)S(1)}, u32[]{:S(2)}, u32[]{:S(2)}) async-start(f32[2,64,96,8]{2,3,0,1:T(8,128)} %copy.59), calls=%async_computation.1 | async-start | bytes 1048576 | tf_op jit(solution)/shard_map/all_to_all | solution.py:183
  318.6 19.7 %all-to-all-start.2 = ((f32[2,8,96,64]{2,0,1,3:T(2,128)}), f32[2,8,96,64]{2,0,1,3:T(2,128)S(1)}, u32[]{:S(2)}, u32[]{:S(2)}) async-start(f32[2,8,96,64]{2,0,1,3:T(2,128)} %copy.65), calls=%async_computation.2 | async-start | bytes 1048576 | tf_op jit(solution)/shard_map/all_to_all | solution.py:187
  340.8 1.9 collective-permute-start.4
  340.9 7.8 %collective-permute-start.5 = (bf16[96,8,128]{2,1,0:T(8,128)(2,1)S(1)}, bf16[96,8,128]{2,1,0:T(8,128)(2,1)S(1)}, u32[]{:S(2)}, u32[]{:S(2)}) collective-permute-start(bf16[96,8,128]{2,1,0:T(8,128)(2,1)S(1)} %get-tuple-element.574), channel_id=1, source_target_pairs={{0,2},{1,3},{2,0},{3,1},{4,6},{5,7},{6,4},{7,5},{8,10},{9,11},{10,... | collective-permute-start | bytes 589832 | tf_op jit(solution)/shard_map/ppermute | solution.py:28
  341.9 9.9 %collective-permute-start.6 = (bf16[96,8,128]{2,1,0:T(8,128)(2,1)S(1)}, bf16[96,8,128]{2,1,0:T(8,128)(2,1)S(1)}, u32[]{:S(2)}, u32[]{:S(2)}) collective-permute-start(bf16[96,8,128]{2,1,0:T(8,128)(2,1)S(1)} %get-tuple-element.573), channel_id=1, source_target_pairs={{0,3},{1,2},{2,1},{3,0},{4,7},{5,6},{6,5},{7,4},{8,11},{9,10},{10,... | collective-permute-start | bytes 589832 | tf_op jit(solution)/shard_map/ppermute | solution.py:28
  (1 other events, 0.6 us)
